TPU v7x, 128 devices: a whole 4x4x4 slice. The times are simulated.
128 devices in a mesh: band: 16 (over z_lo, x, core), col: 8 (over z_hi, y).
Axes of the slice: x: 4, y: 4, z: 4 (z_hi: 2, z_lo: 2; z = z_hi * 2 + z_lo), core: 2. Of those that a mesh axis runs over, the one named last changes fastest.
Arguments:
- bands: float32 [8192, 16384], P(('band', 'col')), may hold values from -6 to 6
- row_interp: float32 [16, 512, 640], P('band'), may hold values from -0.25 to 0.25
- col_interp: float32 [32, 640, 512], P('col'), may hold values from -0.25 to 0.25
- row_start: int32 [16], P('band'), may hold values from 0 to 128
- col_start: int32 [32], P('col'), may hold values from 0 to 128
- spacing: float32 [16], P('band'), may hold values from 0.5 to 2
Outputs:
- elevation: float32 [8192, 16384], P('band', 'col')
- slope_sine: float32 [8192, 16384], P('band', 'col')
- hillshade: float32 [8192, 16384], P('band', 'col')
All inputs are finite; a program needn't handle non-finite values.
Results may differ from a plain program's by a relative error of at most 0.0003.
Values sent between devices are 32-bit elements; how exact they have to be, the bound alone decides.
A program may use at most 128 MiB of HBM per device.

v0:
```python
import jax
import jax.numpy as jnp
from jax import lax
from jax.experimental import pallas as pl
from jax.experimental.pallas import tpu as pltpu
from jax.sharding import PartitionSpec as P

MESH = pl.DeviceIdType.MESH
F32, BF16 = jnp.float32, jnp.bfloat16

TILE, WIN, MARGIN = 512, 640, 128
NB, NC, NT = 16, 8, 4
COLS = 16384
BLOCK = TILE * NT
SPAN = TILE + 2 * MARGIN
EXT = BLOCK + 2 * MARGIN
SRC = TILE // NC
Z = TILE + 16

GROUPS = (
    ((0, 128, 384, 640, 768), 0),
    ((1536, 1664, 1920, 2176, 2304), 3),
    ((768, 1024, 1280), 1),
    ((1280, 1536), 2),
)
HORN = ((), (), ((0, 768), (768, 896), (1664, 2048)), ((896, 1664),))


def split(x):
    high = x.astype(BF16)
    return high, (x - high.astype(F32)).astype(BF16)


def dot(a, b):
    return lax.dot_general(a, b, (((1,), (0,)), ((), ())), preferred_element_type=F32)


def dot3(ah, al, bh, bl):
    return dot(ah, bh) + dot(ah, bl) + dot(al, bh)


def gather_kernel(
    row_start, col_start, spacing, bands, row_interp, col_interp,
    oz, osl, ohi,
    ext, z, rmat, cmat, rh, rl, ch, cl, wh, wl, left, right, lsend, rsend, vz, vs, vh,
    send_sem, recv_sem, own_sem, mat_sem, up_send, up_recv, dn_send, dn_recv,
    eu_send, eu_recv, ed_send, ed_recv, side_send, side_recv, corner_send, corner_recv, out_sem,
):
    b, c = lax.axis_index("band"), lax.axis_index("col")
    zh, y = c // 4, lax.rem(c, 4)

    def peer(s):
        return lax.rem(zh + lax.rem(s, 2), 2) * 4 + lax.rem(y + s // 2, 4)

    def at(db, dc):
        return {"band": b + db, "col": c + dc}

    def exists(db, dc):
        ok = jnp.bool_(True)
        if db < 0:
            ok = b > 0
        if db > 0:
            ok = b < NB - 1
        if dc < 0:
            ok = jnp.logical_and(ok, c > 0)
        if dc > 0:
            ok = jnp.logical_and(ok, c < NC - 1)
        return ok

    z[0:8, :] = jnp.zeros((8, EXT), F32)
    z[Z - 8 : Z, :] = jnp.zeros((8, EXT), F32)
    left[...] = jnp.zeros_like(left)
    right[...] = jnp.zeros_like(right)

    barrier = pltpu.get_barrier_semaphore()

    def greet(s, carry):
        pl.semaphore_signal(barrier, 1, device_id={"col": peer(s)}, device_id_type=MESH)
        return carry

    lax.fori_loop(1, NC, greet, 0)
    near = [(db, dc) for db in (-1, 1) for dc in (-1, 0, 1)]
    for db, dc in near:
        @pl.when(exists(db, dc))
        def _():
            pl.semaphore_signal(barrier, 1, device_id=at(db, dc), device_id_type=MESH)
    rows_near = (b > 0).astype(jnp.int32) + (b < NB - 1).astype(jnp.int32)
    cols_near = (c > 0).astype(jnp.int32) + (c < NC - 1).astype(jnp.int32)
    pl.semaphore_wait(barrier, NC - 1 + rows_near * (1 + cols_near))

    mine = pl.ds(pl.multiple_of(c * SRC, SRC), SRC)
    for g, (edges, _) in enumerate(GROUPS):
        for lo, hi in zip(edges[:-1], edges[1:]):
            def source(dst):
                start = lax.rem(dst * BLOCK + (lo + COLS - MARGIN), COLS)
                return bands.at[:, pl.ds(pl.multiple_of(start, 128), hi - lo)]

            def send(s, carry):
                dst = peer(s)
                pltpu.make_async_remote_copy(
                    source(dst), ext.at[mine, lo:hi], send_sem.at[g], recv_sem.at[g, c],
                    device_id={"col": dst}, device_id_type=MESH,
                ).start()
                return carry

            lax.fori_loop(1, NC, send, 0)
            pltpu.make_async_copy(source(c), ext.at[mine, lo:hi], own_sem.at[g]).start()

    rcopy = pltpu.make_async_copy(row_interp.at[0], rmat, mat_sem.at[0])
    ccopy = pltpu.make_async_copy(col_interp, cmat, mat_sem.at[1])
    rcopy.start()
    ccopy.start()

    @pl.when(b == 0)
    def _():
        ext[TILE : TILE + MARGIN, :] = jnp.zeros((MARGIN, EXT), F32)

    @pl.when(b == NB - 1)
    def _():
        ext[TILE + MARGIN :, :] = jnp.zeros((MARGIN, EXT), F32)

    rcopy.wait()
    ah, al = split(rmat[...])
    r0 = row_start[0]
    for k in range(3):
        m = lax.broadcasted_iota(jnp.int32, (WIN, 256), 1) + k * 256
        row = m + MARGIN if k < 2 else jnp.where(m < TILE + MARGIN, m - TILE, m)
        hot = jnp.where(row - r0 == lax.broadcasted_iota(jnp.int32, (WIN, 256), 0), 1.0, 0.0).astype(BF16)
        rh[:, k * 256 : (k + 1) * 256] = dot(ah, hot).astype(BF16)
        rl[:, k * 256 : (k + 1) * 256] = dot(al, hot).astype(BF16)

    ccopy.wait()
    for j in range(NT):
        c0 = col_start[j]
        low = jnp.where(c == 0, MARGIN, 0) if j == 0 else 0
        high = jnp.where(c == NC - 1, TILE + MARGIN, SPAN) if j == NT - 1 else SPAN

        def move(k, carry):
            base = pl.multiple_of(k * 256, 256)
            ah, al = split(cmat[j])
            m = lax.broadcasted_iota(jnp.int32, (256, WIN), 0) + base
            hit = m - c0 == lax.broadcasted_iota(jnp.int32, (256, WIN), 1)
            hit = jnp.logical_and(hit, jnp.logical_and(m >= low, m < high))
            hot = jnp.where(hit, 1.0, 0.0).astype(BF16)
            ch[j, pl.ds(base, 256), :] = dot(hot, ah).astype(BF16)
            cl[j, pl.ds(base, 256), :] = dot(hot, al).astype(BF16)
            return carry

        lax.fori_loop(0, SPAN // 256, move, 0)

    inv = jnp.tile(1.0 / jnp.full((16, 128), 8.0 * spacing[0], F32), (1, 3))
    outs = []

    def edge(ref_from, ref_to, sends, recvs, db, dc):
        return pltpu.make_async_remote_copy(
            ref_from, ref_to, sends, recvs, device_id=at(db, dc), device_id_type=MESH
        )

    waits = []
    for g, (edges, tile) in enumerate(GROUPS):
        lo, hi = edges[0], edges[-1]
        cols = slice(lo, hi)

        def arrive(s, carry):
            src = peer(s)
            rows = ext.at[pl.ds(pl.multiple_of(src * SRC, SRC), SRC), cols]
            pltpu.make_async_remote_copy(
                rows, rows, send_sem.at[g], recv_sem.at[g, src], device_id={"col": src}, device_id_type=MESH
            ).wait_recv()
            return carry

        lax.fori_loop(1, NC, arrive, 0)
        pltpu.make_async_copy(ext.at[mine, cols], ext.at[mine, cols], own_sem.at[g]).wait()

        down = edge(ext.at[TILE - MARGIN : TILE, cols], ext.at[TILE : TILE + MARGIN, cols], dn_send.at[g], dn_recv.at[g], 1, 0)
        upward = edge(ext.at[0:MARGIN, cols], ext.at[TILE + MARGIN : SPAN, cols], up_send.at[g], up_recv.at[g], -1, 0)
        pl.when(b < NB - 1)(down.start)
        pl.when(b > 0)(upward.start)
        pl.when(b > 0)(down.wait_recv)
        pl.when(b < NB - 1)(upward.wait_recv)

        def rows_of(n, carry):
            at_n = pl.ds(pl.multiple_of(lo + n * 256, 256), 256)
            xh, xl = split(ext[:, at_n])
            part = dot3(rh[...], rl[...], xh, xl)
            high, low = split(part)
            wh[:, at_n] = high
            wl[:, at_n] = low
            return carry

        lax.fori_loop(0, (hi - lo) // 256, rows_of, 0)

        def cols_of(n, carry):
            at_n = pl.ds(pl.multiple_of(n * 256, 256), 256)
            part = dot3(wh[:, tile * TILE : tile * TILE + SPAN], wl[:, tile * TILE : tile * TILE + SPAN], ch[tile, :, at_n], cl[tile, :, at_n])
            z[8 : 8 + TILE, pl.ds(pl.multiple_of(MARGIN + tile * TILE + n * 256, 128), 256)] = part
            return carry

        lax.fori_loop(0, TILE // 256, cols_of, 0)

        tc = slice(MARGIN + tile * TILE, MARGIN + (tile + 1) * TILE)
        first, last = slice(8, 16), slice(TILE, TILE + 8)
        top, bottom = slice(0, 8), slice(Z - 8, Z)
        pairs = [
            (edge(z.at[last, tc], z.at[top, tc], ed_send.at[tile], ed_recv.at[tile], 1, 0), (1, 0)),
            (edge(z.at[first, tc], z.at[bottom, tc], eu_send.at[tile], eu_recv.at[tile], -1, 0), (-1, 0)),
        ]
        if tile == 0:
            near_cols, far_cols, dc = slice(MARGIN, 2 * MARGIN), slice(EXT - MARGIN, EXT), -1
            lsend[...] = jnp.transpose(z[8 : 8 + TILE, near_cols])[0:8, :]
            pairs.append((edge(lsend, right.at[0:8, :], side_send.at[0], side_recv.at[0], 0, -1), (0, -1)))
        if tile == NT - 1:
            near_cols, far_cols, dc = slice(BLOCK, BLOCK + MARGIN), slice(0, MARGIN), 1
            rsend[...] = jnp.transpose(z[8 : 8 + TILE, near_cols])[120:128, :]
            pairs.append((edge(rsend, left.at[120:128, :], side_send.at[1], side_recv.at[1], 0, 1), (0, 1)))
        if tile in (0, NT - 1):
            i = 0 if tile == 0 else 2
            pairs.append((edge(z.at[last, near_cols], z.at[top, far_cols], corner_send.at[i], corner_recv.at[i], 1, dc), (1, dc)))
            pairs.append((edge(z.at[first, near_cols], z.at[bottom, far_cols], corner_send.at[i + 1], corner_recv.at[i + 1], -1, dc), (-1, dc)))
        for copy, way in pairs:
            pl.when(exists(*way))(copy.start)
        waits.extend(pairs)

        if not HORN[g]:
            continue
        for copy, way in waits:
            pl.when(exists(-way[0], -way[1]))(copy.wait_recv)
            pl.when(exists(*way))(copy.wait_send)
        waits = []
        if g == 2:
            z[8 : 8 + TILE, 0:MARGIN] = jnp.transpose(left[...])
            z[8 : 8 + TILE, EXT - MARGIN : EXT] = jnp.transpose(right[...])
        for first_col, last_col in HORN[g]:
            width = 384 if (last_col - first_col) % 384 == 0 else 128
            span = width + 256

            def strip(i, carry):
                r = pl.multiple_of(i * 16, 16)

                def chunk(n, carry):
                    at_n = pl.multiple_of(first_col + n * width, 128)
                    blk = z[pl.ds(r, 32), pl.ds(at_n, span)]
                    up, mid, dn = blk[7:23], blk[8:24], blk[9:25]
                    s = up + dn + 2.0 * mid
                    d = dn - up
                    sc = inv[:, :width]
                    p = (pltpu.roll(s, span - 1, 1) - pltpu.roll(s, 1, 1))[:, 128 : 128 + width] * sc
                    q = (pltpu.roll(d, span - 1, 1) + pltpu.roll(d, 1, 1) + 2.0 * d)[:, 128 : 128 + width] * sc
                    t = p * p + q * q
                    f = lax.rsqrt(1.0 + t)
                    o = (pl.ds(r, 16), pl.ds(at_n, width))
                    vz[o] = mid[:, 128 : 128 + width]
                    vs[o] = jnp.sqrt(t) * f
                    vh[o] = (0.70710678 + 0.5 * (q - p)) * f
                    return carry

                return lax.fori_loop(0, (last_col - first_col) // width, chunk, carry)

            lax.fori_loop(0, TILE // 16, strip, 0)
            cs = slice(first_col, last_col)
            for k, (v, o) in enumerate(((vz, oz), (vs, osl), (vh, ohi))):
                copy = pltpu.make_async_copy(v.at[:, cs], o.at[:, cs], out_sem.at[len(outs)])
                copy.start()
                outs.append(copy)

    for g, (edges, _) in enumerate(GROUPS):
        lo, hi = edges[0], edges[-1]
        cols = slice(lo, hi)
        gone = ext.at[0 : (NC - 1) * SRC, cols]
        pltpu.make_async_remote_copy(
            gone, gone, send_sem.at[g], recv_sem.at[g, c], device_id={"col": peer(1)}, device_id_type=MESH
        ).wait_send()
        down = edge(ext.at[TILE - MARGIN : TILE, cols], ext.at[TILE : TILE + MARGIN, cols], dn_send.at[g], dn_recv.at[g], 1, 0)
        upward = edge(ext.at[0:MARGIN, cols], ext.at[TILE + MARGIN : SPAN, cols], up_send.at[g], up_recv.at[g], -1, 0)
        pl.when(b < NB - 1)(down.wait_send)
        pl.when(b > 0)(upward.wait_send)
    for copy in outs:
        copy.wait()


def on_device(bands, row_interp, col_interp, row_start, col_start, spacing):
    out = jax.ShapeDtypeStruct((TILE, BLOCK), F32)
    smem, anywhere = pl.BlockSpec(memory_space=pltpu.SMEM), pl.BlockSpec(memory_space=pl.ANY)
    vmem, dma = pltpu.VMEM, pltpu.SemaphoreType.DMA
    ng = len(GROUPS)
    return pl.pallas_call(
        gather_kernel,
        out_shape=(out,) * 3,
        in_specs=[smem] * 3 + [anywhere] * 3,
        out_specs=(anywhere,) * 3,
        scratch_shapes=[
            vmem((SPAN, EXT), F32), vmem((Z, EXT), F32),
            vmem((TILE, WIN), F32), vmem((NT, WIN, TILE), F32),
            vmem((TILE, SPAN), BF16), vmem((TILE, SPAN), BF16),
            vmem((NT, SPAN, TILE), BF16), vmem((NT, SPAN, TILE), BF16),
            vmem((TILE, EXT), BF16), vmem((TILE, EXT), BF16),
            vmem((MARGIN, TILE), F32), vmem((MARGIN, TILE), F32),
            vmem((8, TILE), F32), vmem((8, TILE), F32),
            vmem((TILE, BLOCK), F32), vmem((TILE, BLOCK), F32), vmem((TILE, BLOCK), F32),
            dma((ng,)), dma((ng, NC)), dma((ng,)), dma((2,)),
            dma((ng,)), dma((ng,)), dma((ng,)), dma((ng,)),
            dma((NT,)), dma((NT,)), dma((NT,)), dma((NT,)),
            dma((2,)), dma((2,)), dma((4,)), dma((4,)), dma((12,)),
        ],
        compiler_params=pltpu.CompilerParams(
            collective_id=0, has_side_effects=True, vmem_limit_bytes=60 * 2**20
        ),
    )(row_start, col_start, spacing, bands, row_interp, col_interp)


def solution(mesh):
    in_specs = (
        P(("band", "col"), None),
        P("band", None, None),
        P("col", None, None),
        P("band"),
        P("col"),
        P("band"),
    )
    out_specs = (P("band", "col"), P("band", "col"), P("band", "col"))
    return jax.shard_map(
        on_device, mesh=mesh, in_specs=in_specs, out_specs=out_specs, check_vma=False
    )
```

profile of v0, /device:TPU:101, one launch (start us, length us, event | category | flops | bytes accessed | tf_op | source)
XLA Modules:
  0.0 135.1 jit_solution(6990087618018672559)
XLA Ops:
  1.9 122.6 %shard_map.85 = (f32[512,2048]{1,0:T(8,128)}, f32[512,2048]{1,0:T(8,128)}, f32[512,2048]{1,0:T(8,128)}) custom-call(s32[1]{0:T(128)S(6)} %copy.12.row_start, s32[4]{0:T(128)} %col_start.1, f32[1]{0:T(128)S(6)} %copy.13.spacing, f32[64,16384]{1,0:T(8,128)} %bands.1, f32[1,512,640]{2,1,0:T(8,128)} %row_interp.1, f32[4,640,512]{2,1,0:T(8,128)} %col_interp.1), custom_call_target="tpu_custom_call" | custom-call | tf_op jit(solution)/shard_map/pallas_call | solution.py:286
  124.6 0.0 copy-start.1
  124.6 4.8 %copy.14 = f32[512,2048]{1,0:T(8,128)} copy(f32[512,2048]{1,0:T(8,128)} %get-tuple-element.6) | data formatting | bytes 8388608
  129.4 0.0 copy-done.1
  129.4 0.0 copy-start
  129.4 2.1 %copy.15 = f32[512,2048]{1,0:T(8,128)} copy(f32[512,2048]{1,0:T(8,128)S(1)} %copy-done.1) | data formatting | bytes 8388608
  131.6 1.6 %copy-done = f32[512,2048]{1,0:T(8,128)S(1)} copy-done((f32[512,2048]{1,0:T(8,128)S(1)}, f32[512,2048]{1,0:T(8,128)}, u32[]{:S(2)}) %copy-start) | copy-done | bytes 4194328
  133.1 2.0 %copy.16 = f32[512,2048]{1,0:T(8,128)} copy(f32[512,2048]{1,0:T(8,128)S(1)} %copy-done) | data formatting | bytes 8388608
Async XLA Ops:
  124.6 4.9 %copy-start.1 = (f32[512,2048]{1,0:T(8,128)S(1)}, f32[512,2048]{1,0:T(8,128)}, u32[]{:S(2)}) copy-start(f32[512,2048]{1,0:T(8,128)} %get-tuple-element.7) | copy-start | bytes 12582916
  129.4 3.7 %copy-start = (f32[512,2048]{1,0:T(8,128)S(1)}, f32[512,2048]{1,0:T(8,128)}, u32[]{:S(2)}) copy-start(f32[512,2048]{1,0:T(8,128)} %get-tuple-element.8) | copy-start | bytes 12582916
where the time goes:
time: 135 us
  Pallas kernels  123 us (91%)
  local copies, waits for them, and re-layouts  10.6 us (8%)
  between operations  1.94 us (1%)
    pallas_call x1, Pallas kernels, on_device(): pl.pallas_call(gather_kernel, out_shape=(out,) * 3, in_specs=[smem] * 3 +...  123 us
    unnamed x7, local copies, waits for them, and re-layouts  10.6 us

commit v1 on v0

--- a/solution.py
+++ b/solution.py
@@ -17,13 +17,21 @@
 SRC = TILE // NC
 Z = TILE + 16
 
-GROUPS = (
-    ((0, 128, 384, 640, 768), 0),
-    ((1536, 1664, 1920, 2176, 2304), 3),
-    ((768, 1024, 1280), 1),
-    ((1280, 1536), 2),
+UNITS = (
+    (0, 128, 256),
+    (256, 512, 768),
+    (1536, 1792),
+    (1792, 2048, 2176, 2304),
+    (768, 1024),
+    (1024, 1280),
+    (1280, 1536),
 )
-HORN = ((), (), ((0, 768), (768, 896), (1664, 2048)), ((896, 1664),))
+AHEAD = 3
+DONE = {1: 0, 3: 3, 5: 1, 6: 2}
+HORN = {3: (0, ((128, 384),)), 1: (3, ((0, 128), (1664, 2048))), 2: (1, ((384, 896),))}
+LATE = (896, 1664)
+KERNEL_VMEM = 47 * 2**20
+TINY = 1.1754944e-38
 
 
 def split(x):
@@ -39,12 +47,32 @@
     return dot(ah, bh) + dot(ah, bl) + dot(al, bh)
 
 
+def horn(z, inv, r, lo, width):
+    span = width + 2 * MARGIN
+    blk = z[pl.ds(r, 32), lo : lo + span]
+    up, mid, dn = blk[7:23], blk[8:24], blk[9:25]
+    s = up + dn + 2.0 * mid
+    d = dn - up
+    sc = jnp.tile(inv, (1, width // 128))
+    keep = slice(MARGIN, MARGIN + width)
+    p = (pltpu.roll(s, span - 1, 1) - pltpu.roll(s, 1, 1))[:, keep] * sc
+    q = (pltpu.roll(d, span - 1, 1) + pltpu.roll(d, 1, 1) + 2.0 * d)[:, keep] * sc
+    t = p * p + q * q
+    u = 1.0 + t
+    f = lax.rsqrt(u)
+    return t * lax.rsqrt(jnp.maximum(t * u, TINY)), (0.70710678 + 0.5 * (q - p)) * f
+
+
+def inverse(spacing):
+    return 1.0 / jnp.full((16, 128), 8.0 * spacing[0], F32)
+
+
 def gather_kernel(
     row_start, col_start, spacing, bands, row_interp, col_interp,
-    oz, osl, ohi,
-    ext, z, rmat, cmat, rh, rl, ch, cl, wh, wl, left, right, lsend, rsend, vz, vs, vh,
+    z, vs, vh,
+    ext, rmat, cmat, rh, rl, ch, cl, wh, wl, left, right, lsend, rsend,
     send_sem, recv_sem, own_sem, mat_sem, up_send, up_recv, dn_send, dn_recv,
-    eu_send, eu_recv, ed_send, ed_recv, side_send, side_recv, corner_send, corner_recv, out_sem,
+    eu_send, eu_recv, ed_send, ed_recv, side_send, side_recv, corner_send, corner_recv,
 ):
     b, c = lax.axis_index("band"), lax.axis_index("col")
     zh, y = c // 4, lax.rem(c, 4)
@@ -89,13 +117,14 @@
     pl.semaphore_wait(barrier, NC - 1 + rows_near * (1 + cols_near))
 
     mine = pl.ds(pl.multiple_of(c * SRC, SRC), SRC)
-    for g, (edges, _) in enumerate(GROUPS):
+    def post(g):
+        edges = UNITS[g]
         for lo, hi in zip(edges[:-1], edges[1:]):
-            def source(dst):
+            def source(dst, lo=lo, hi=hi):
                 start = lax.rem(dst * BLOCK + (lo + COLS - MARGIN), COLS)
                 return bands.at[:, pl.ds(pl.multiple_of(start, 128), hi - lo)]
 
-            def send(s, carry):
+            def send(s, carry, lo=lo, hi=hi, source=source):
                 dst = peer(s)
                 pltpu.make_async_remote_copy(
                     source(dst), ext.at[mine, lo:hi], send_sem.at[g], recv_sem.at[g, c],
@@ -105,6 +134,9 @@
 
             lax.fori_loop(1, NC, send, 0)
             pltpu.make_async_copy(source(c), ext.at[mine, lo:hi], own_sem.at[g]).start()
+
+    for g in range(AHEAD):
+        post(g)
 
     rcopy = pltpu.make_async_copy(row_interp.at[0], rmat, mat_sem.at[0])
     ccopy = pltpu.make_async_copy(col_interp, cmat, mat_sem.at[1])
@@ -148,20 +180,23 @@
 
         lax.fori_loop(0, SPAN // 256, move, 0)
 
-    inv = jnp.tile(1.0 / jnp.full((16, 128), 8.0 * spacing[0], F32), (1, 3))
-    outs = []
+    inv = inverse(spacing)
 
     def edge(ref_from, ref_to, sends, recvs, db, dc):
         return pltpu.make_async_remote_copy(
             ref_from, ref_to, sends, recvs, device_id=at(db, dc), device_id_type=MESH
         )
 
-    waits = []
-    for g, (edges, tile) in enumerate(GROUPS):
-        lo, hi = edges[0], edges[-1]
-        cols = slice(lo, hi)
-
-        def arrive(s, carry):
+    def relays(g):
+        cols = slice(UNITS[g][0], UNITS[g][-1])
+        down = edge(ext.at[TILE - MARGIN : TILE, cols], ext.at[TILE : TILE + MARGIN, cols], dn_send.at[g], dn_recv.at[g], 1, 0)
+        upward = edge(ext.at[0:MARGIN, cols], ext.at[TILE + MARGIN : SPAN, cols], up_send.at[g], up_recv.at[g], -1, 0)
+        return down, upward
+
+    def arrive(g):
+        cols = slice(UNITS[g][0], UNITS[g][-1])
+
+        def one(s, carry):
             src = peer(s)
             rows = ext.at[pl.ds(pl.multiple_of(src * SRC, SRC), SRC), cols]
             pltpu.make_async_remote_copy(
@@ -169,13 +204,27 @@
             ).wait_recv()
             return carry
 
-        lax.fori_loop(1, NC, arrive, 0)
+        lax.fori_loop(1, NC, one, 0)
         pltpu.make_async_copy(ext.at[mine, cols], ext.at[mine, cols], own_sem.at[g]).wait()
-
-        down = edge(ext.at[TILE - MARGIN : TILE, cols], ext.at[TILE : TILE + MARGIN, cols], dn_send.at[g], dn_recv.at[g], 1, 0)
-        upward = edge(ext.at[0:MARGIN, cols], ext.at[TILE + MARGIN : SPAN, cols], up_send.at[g], up_recv.at[g], -1, 0)
+        down, upward = relays(g)
         pl.when(b < NB - 1)(down.start)
         pl.when(b > 0)(upward.start)
+        if g + AHEAD < len(UNITS):
+            post(g + AHEAD)
+
+    def finish(pairs):
+        for copy, way in pairs:
+            pl.when(exists(-way[0], -way[1]))(copy.wait_recv)
+            pl.when(exists(*way))(copy.wait_send)
+
+    waits = {}
+    arrive(0)
+    for g in range(len(UNITS)):
+        lo, hi = UNITS[g][0], UNITS[g][-1]
+        tile = DONE.get(g)
+        if g + 1 < len(UNITS):
+            arrive(g + 1)
+        down, upward = relays(g)
         pl.when(b > 0)(down.wait_recv)
         pl.when(b < NB - 1)(upward.wait_recv)
 
@@ -189,6 +238,8 @@
             return carry
 
         lax.fori_loop(0, (hi - lo) // 256, rows_of, 0)
+        if tile is None:
+            continue
 
         def cols_of(n, carry):
             at_n = pl.ds(pl.multiple_of(n * 256, 256), 256)
@@ -219,62 +270,62 @@
             pairs.append((edge(z.at[first, near_cols], z.at[bottom, far_cols], corner_send.at[i + 1], corner_recv.at[i + 1], -1, dc), (-1, dc)))
         for copy, way in pairs:
             pl.when(exists(*way))(copy.start)
-        waits.extend(pairs)
-
-        if not HORN[g]:
+        waits[tile] = pairs
+
+        if tile not in HORN:
             continue
-        for copy, way in waits:
-            pl.when(exists(-way[0], -way[1]))(copy.wait_recv)
-            pl.when(exists(*way))(copy.wait_send)
-        waits = []
-        if g == 2:
+        ready, spans = HORN[tile]
+        finish(waits.pop(ready))
+        if ready == 3:
             z[8 : 8 + TILE, 0:MARGIN] = jnp.transpose(left[...])
             z[8 : 8 + TILE, EXT - MARGIN : EXT] = jnp.transpose(right[...])
-        for first_col, last_col in HORN[g]:
-            width = 384 if (last_col - first_col) % 384 == 0 else 128
-            span = width + 256
-
-            def strip(i, carry):
-                r = pl.multiple_of(i * 16, 16)
-
-                def chunk(n, carry):
-                    at_n = pl.multiple_of(first_col + n * width, 128)
-                    blk = z[pl.ds(r, 32), pl.ds(at_n, span)]
-                    up, mid, dn = blk[7:23], blk[8:24], blk[9:25]
-                    s = up + dn + 2.0 * mid
-                    d = dn - up
-                    sc = inv[:, :width]
-                    p = (pltpu.roll(s, span - 1, 1) - pltpu.roll(s, 1, 1))[:, 128 : 128 + width] * sc
-                    q = (pltpu.roll(d, span - 1, 1) + pltpu.roll(d, 1, 1) + 2.0 * d)[:, 128 : 128 + width] * sc
-                    t = p * p + q * q
-                    f = lax.rsqrt(1.0 + t)
-                    o = (pl.ds(r, 16), pl.ds(at_n, width))
-                    vz[o] = mid[:, 128 : 128 + width]
-                    vs[o] = jnp.sqrt(t) * f
-                    vh[o] = (0.70710678 + 0.5 * (q - p)) * f
-                    return carry
-
-                return lax.fori_loop(0, (last_col - first_col) // width, chunk, carry)
-
-            lax.fori_loop(0, TILE // 16, strip, 0)
-            cs = slice(first_col, last_col)
-            for k, (v, o) in enumerate(((vz, oz), (vs, osl), (vh, ohi))):
-                copy = pltpu.make_async_copy(v.at[:, cs], o.at[:, cs], out_sem.at[len(outs)])
-                copy.start()
-                outs.append(copy)
-
-    for g, (edges, _) in enumerate(GROUPS):
-        lo, hi = edges[0], edges[-1]
-        cols = slice(lo, hi)
+
+        def strip(i, carry):
+            r = pl.multiple_of(i * 16, 16)
+            for first_col, last_col in spans:
+                o = (pl.ds(r, 16), slice(first_col, last_col))
+                vs[o], vh[o] = horn(z, inv, r, first_col, last_col - first_col)
+            return carry
+
+        lax.fori_loop(0, TILE // 16, strip, 0)
+
+    for pairs in waits.values():
+        finish(pairs)
+    for g in range(len(UNITS)):
+        cols = slice(UNITS[g][0], UNITS[g][-1])
         gone = ext.at[0 : (NC - 1) * SRC, cols]
         pltpu.make_async_remote_copy(
             gone, gone, send_sem.at[g], recv_sem.at[g, c], device_id={"col": peer(1)}, device_id_type=MESH
         ).wait_send()
-        down = edge(ext.at[TILE - MARGIN : TILE, cols], ext.at[TILE : TILE + MARGIN, cols], dn_send.at[g], dn_recv.at[g], 1, 0)
-        upward = edge(ext.at[0:MARGIN, cols], ext.at[TILE + MARGIN : SPAN, cols], up_send.at[g], up_recv.at[g], -1, 0)
+        down, upward = relays(g)
         pl.when(b < NB - 1)(down.wait_send)
         pl.when(b > 0)(upward.wait_send)
-    for copy in outs:
+
+
+def write_kernel(spacing, z, vs, vh, oz, osl, ohi, hs, hh, sem, late_sem):
+    copies = [pltpu.make_async_copy(z.at[8 : 8 + TILE, MARGIN : MARGIN + BLOCK], oz, sem.at[4])]
+    for k, (v, o) in enumerate(((vs, osl), (vh, ohi))):
+        for n, cs in enumerate((slice(0, LATE[0]), slice(LATE[1], BLOCK))):
+            copies.append(pltpu.make_async_copy(v.at[:, cs], o.at[:, cs], sem.at[2 * k + n]))
+    for copy in copies:
+        copy.start()
+    inv = inverse(spacing)
+    parts = 4
+    for part in range(parts):
+        def strip(i, carry):
+            r = pl.multiple_of(i * 16, 16)
+            for lo in range(LATE[0], LATE[1], 384):
+                o = (pl.ds(r, 16), slice(lo - LATE[0], lo - LATE[0] + 384))
+                hs[o], hh[o] = horn(z, inv, r, lo, 384)
+            return carry
+
+        first, last = part * TILE // parts, (part + 1) * TILE // parts
+        lax.fori_loop(first // 16, last // 16, strip, 0)
+        for k, (v, o) in enumerate(((hs, osl), (hh, ohi))):
+            copy = pltpu.make_async_copy(v.at[first:last], o.at[first:last, LATE[0] : LATE[1]], late_sem.at[k, part])
+            copy.start()
+            copies.append(copy)
+    for copy in copies:
         copy.wait()
 
 
@@ -282,30 +333,41 @@
     out = jax.ShapeDtypeStruct((TILE, BLOCK), F32)
     smem, anywhere = pl.BlockSpec(memory_space=pltpu.SMEM), pl.BlockSpec(memory_space=pl.ANY)
     vmem, dma = pltpu.VMEM, pltpu.SemaphoreType.DMA
-    ng = len(GROUPS)
-    return pl.pallas_call(
+    nu = len(UNITS)
+    in_vmem = pl.BlockSpec(memory_space=pltpu.VMEM)
+    z, vs, vh = pl.pallas_call(
         gather_kernel,
-        out_shape=(out,) * 3,
+        out_shape=(vmem((Z, EXT), F32), vmem((TILE, BLOCK), F32), vmem((TILE, BLOCK), F32)),
         in_specs=[smem] * 3 + [anywhere] * 3,
-        out_specs=(anywhere,) * 3,
+        out_specs=(in_vmem,) * 3,
         scratch_shapes=[
-            vmem((SPAN, EXT), F32), vmem((Z, EXT), F32),
+            vmem((SPAN, EXT), F32),
             vmem((TILE, WIN), F32), vmem((NT, WIN, TILE), F32),
             vmem((TILE, SPAN), BF16), vmem((TILE, SPAN), BF16),
             vmem((NT, SPAN, TILE), BF16), vmem((NT, SPAN, TILE), BF16),
             vmem((TILE, EXT), BF16), vmem((TILE, EXT), BF16),
             vmem((MARGIN, TILE), F32), vmem((MARGIN, TILE), F32),
             vmem((8, TILE), F32), vmem((8, TILE), F32),
-            vmem((TILE, BLOCK), F32), vmem((TILE, BLOCK), F32), vmem((TILE, BLOCK), F32),
-            dma((ng,)), dma((ng, NC)), dma((ng,)), dma((2,)),
-            dma((ng,)), dma((ng,)), dma((ng,)), dma((ng,)),
+            dma((nu,)), dma((nu, NC)), dma((nu,)), dma((2,)),
+            dma((nu,)), dma((nu,)), dma((nu,)), dma((nu,)),
             dma((NT,)), dma((NT,)), dma((NT,)), dma((NT,)),
-            dma((2,)), dma((2,)), dma((4,)), dma((4,)), dma((12,)),
+            dma((2,)), dma((2,)), dma((4,)), dma((4,)),
         ],
         compiler_params=pltpu.CompilerParams(
-            collective_id=0, has_side_effects=True, vmem_limit_bytes=60 * 2**20
+            collective_id=0, has_side_effects=True, vmem_limit_bytes=KERNEL_VMEM
         ),
     )(row_start, col_start, spacing, bands, row_interp, col_interp)
+    return pl.pallas_call(
+        write_kernel,
+        out_shape=(out,) * 3,
+        in_specs=[smem] + [in_vmem] * 3,
+        out_specs=(anywhere,) * 3,
+        scratch_shapes=[
+            vmem((TILE, LATE[1] - LATE[0]), F32), vmem((TILE, LATE[1] - LATE[0]), F32),
+            dma((5,)), dma((2, 4)),
+        ],
+        compiler_params=pltpu.CompilerParams(vmem_limit_bytes=8 * 2**20),
+    )(spacing, z, vs, vh)
 
 
 def solution(mesh):

time: 135 us -> 103 us (0.76)
  the two profiles are of different devices: /device:TPU:101 before, /device:TPU:109 now
where the time goes in v1:
time: 103 us
  Pallas kernels  101 us (98%)
  between operations  1.93 us (2%)
    pallas_call x1, Pallas kernels, on_device(): pl.pallas_call(gather_kernel, out_shape=(vmem((Z, EXT), F32), vmem((TILE,...  94.8 us
    pallas_call x1, Pallas kernels, on_device(): pl.pallas_call(write_kernel, out_shape=(out,) * 3, in_specs=[smem] + [in_...  6.02 us

profile of v1, /device:TPU:109, one launch (start us, length us, event | category | flops | bytes accessed | tf_op | source)
XLA Modules:
  0.0 102.8 jit_solution(13837033963245099516)
XLA Ops:
  1.9 94.8 %shard_map.85 = (f32[528,2304]{1,0:T(8,128)S(1)}, f32[512,2048]{1,0:T(8,128)S(1)}, f32[512,2048]{1,0:T(8,128)S(1)}) custom-call(s32[1]{0:T(128)S(6)} %copy.9.row_start, s32[4]{0:T(128)} %col_start.1, f32[1]{0:T(128)S(6)} %copy.10.spacing, f32[64,16384]{1,0:T(8,128)} %bands.1, f32[1,512,640]{2,1,0:T(8,128)} %row_interp.1, f32[4,640,512]{2,1,0:T(8,128)} %col_interp.1), custom_call_target="tpu_custom_call" | custom-call | tf_op jit(solution)/shard_map/pallas_call | solution.py:338
  96.8 6.0 %shard_map.86 = (f32[512,2048]{1,0:T(8,128)}, f32[512,2048]{1,0:T(8,128)}, f32[512,2048]{1,0:T(8,128)}) custom-call(f32[1]{0:T(128)S(6)} %copy.10.spacing, f32[528,2304]{1,0:T(8,128)S(1)} %get-tuple-element.6.z, f32[512,2048]{1,0:T(8,128)S(1)} %get-tuple-element.7.vs, f32[512,2048]{1,0:T(8,128)S(1)} %get-tuple-element.8.vh), custom_call_target="tpu_custom_call" | custom-call | tf_op jit(solution)/shard_map/pallas_call | solution.py:360

commit v2 on v1

--- a/solution.py
+++ b/solution.py
@@ -19,17 +19,26 @@
 
 UNITS = (
     (0, 128, 256),
-    (256, 512, 768),
+    (256, 512),
+    (512, 768),
     (1536, 1792),
-    (1792, 2048, 2176, 2304),
+    (1792, 2048),
+    (2048, 2176, 2304),
     (768, 1024),
     (1024, 1280),
     (1280, 1536),
 )
-AHEAD = 3
-DONE = {1: 0, 3: 3, 5: 1, 6: 2}
-HORN = {3: (0, ((128, 384),)), 1: (3, ((0, 128), (1664, 2048))), 2: (1, ((384, 896),))}
+WIDE = 256
+AHEAD = 2
+DONE = {2: 0, 5: 3, 7: 1, 8: 2}
+MAKE = {0: 0, 1: 3, 2: 1, 3: 2}
+HORN = {4: (0, ((128, 384),)), 6: (3, ((0, 128), (1664, 2048))), 8: (1, ((384, 896),))}
 LATE = (896, 1664)
+FROM = NB // 2 - 1
+PARTS = 4
+SLICE = MARGIN // PARTS
+VIA_DOWN = (10, 12, 14)
+VIA_UP = (1, 3, 5)
 KERNEL_VMEM = 47 * 2**20
 TINY = 1.1754944e-38
 
@@ -70,9 +79,9 @@
 def gather_kernel(
     row_start, col_start, spacing, bands, row_interp, col_interp,
     z, vs, vh,
-    ext, rmat, cmat, rh, rl, ch, cl, wh, wl, left, right, lsend, rsend,
+    ext, rmat, cmat, rh, rl, ch, cl, wh, wl, left, right, lsend, rsend, hold, acc,
     send_sem, recv_sem, own_sem, mat_sem, up_send, up_recv, dn_send, dn_recv,
-    eu_send, eu_recv, ed_send, ed_recv, side_send, side_recv, corner_send, corner_recv,
+    eu_send, eu_recv, ed_send, ed_recv, side_send, side_recv, corner_send, corner_recv, hold_send, hold_recv,
 ):
     b, c = lax.axis_index("band"), lax.axis_index("col")
     zh, y = c // 4, lax.rem(c, 4)
@@ -112,9 +121,22 @@
         @pl.when(exists(db, dc))
         def _():
             pl.semaphore_signal(barrier, 1, device_id=at(db, dc), device_id_type=MESH)
+    via_down = jnp.logical_and(b >= VIA_DOWN[0], jnp.logical_and(b <= VIA_DOWN[-1], lax.rem(b, 2) == 0))
+    via_up = jnp.logical_and(b <= VIA_UP[-1], lax.rem(b, 2) == 1)
+    via = jnp.logical_or(via_down, via_up)
+    ends = jnp.logical_or(b == FROM, b == FROM + 1)
+    for other in (FROM, FROM + 1):
+        @pl.when(via)
+        def _():
+            pl.semaphore_signal(barrier, 1, device_id={"band": other, "col": c}, device_id_type=MESH)
+    for other in VIA_DOWN + VIA_UP:
+        @pl.when(ends)
+        def _():
+            pl.semaphore_signal(barrier, 1, device_id={"band": other, "col": c}, device_id_type=MESH)
+    extra = 2 * via.astype(jnp.int32) + 6 * ends.astype(jnp.int32)
     rows_near = (b > 0).astype(jnp.int32) + (b < NB - 1).astype(jnp.int32)
     cols_near = (c > 0).astype(jnp.int32) + (c < NC - 1).astype(jnp.int32)
-    pl.semaphore_wait(barrier, NC - 1 + rows_near * (1 + cols_near))
+    pl.semaphore_wait(barrier, NC - 1 + rows_near * (1 + cols_near) + extra)
 
     mine = pl.ds(pl.multiple_of(c * SRC, SRC), SRC)
     def post(g):
@@ -161,8 +183,9 @@
         rh[:, k * 256 : (k + 1) * 256] = dot(ah, hot).astype(BF16)
         rl[:, k * 256 : (k + 1) * 256] = dot(al, hot).astype(BF16)
 
-    ccopy.wait()
-    for j in range(NT):
+    def make(j):
+        if j == MAKE[0]:
+            ccopy.wait()
         c0 = col_start[j]
         low = jnp.where(c == 0, MARGIN, 0) if j == 0 else 0
         high = jnp.where(c == NC - 1, TILE + MARGIN, SPAN) if j == NT - 1 else SPAN
@@ -207,10 +230,52 @@
         lax.fori_loop(1, NC, one, 0)
         pltpu.make_async_copy(ext.at[mine, cols], ext.at[mine, cols], own_sem.at[g]).wait()
         down, upward = relays(g)
-        pl.when(b < NB - 1)(down.start)
-        pl.when(b > 0)(upward.start)
+        if g == len(UNITS) - 1:
+            pl.when(b < NB - 1)(down.start)
+            pl.when(b > 0)(upward.start)
+        else:
+            pl.when(jnp.logical_and(b < NB - 1, b != FROM))(down.start)
+            pl.when(jnp.logical_and(b > 0, b != FROM + 1))(upward.start)
+            for at_band, base, to, direct, others, sends, recvs in (
+                (FROM, TILE - MARGIN, TILE, FROM + 1, VIA_DOWN, dn_send, dn_recv),
+                (FROM + 1, 0, TILE + MARGIN, FROM, VIA_UP, up_send, up_recv),
+            ):
+                @pl.when(b == at_band)
+                def _():
+                    for i in range(PARTS):
+                        part = slice(base + i * SLICE, base + (i + 1) * SLICE)
+                        pltpu.make_async_remote_copy(
+                            ext.at[part, cols],
+                            hold.at[:, cols] if i else ext.at[to : to + SLICE, cols],
+                            sends.at[g], hold_recv.at[g] if i else recvs.at[g],
+                            device_id={"band": others[i - 1] if i else direct, "col": c}, device_id_type=MESH,
+                        ).start()
         if g + AHEAD < len(UNITS):
             post(g + AHEAD)
+
+    def forwards(g):
+        cols = slice(UNITS[g][0], UNITS[g][-1])
+        made = []
+        for to, start, dest, recvs in (
+            (FROM + 1, TILE + (b - FROM - 1) // 2 * SLICE, via_down, dn_recv),
+            (FROM, TILE + MARGIN + (b + 1) // 2 * SLICE, via_up, up_recv),
+        ):
+            copy = pltpu.make_async_remote_copy(
+                hold.at[:, cols], ext.at[pl.ds(pl.multiple_of(start, SLICE), SLICE), cols], hold_send.at[g], recvs.at[g],
+                device_id={"band": to, "col": c}, device_id_type=MESH,
+            )
+            made.append((dest, copy))
+        return made
+
+    def forward(g):
+        for chosen, copy in forwards(g):
+            @pl.when(chosen)
+            def _():
+                pltpu.make_async_remote_copy(
+                    hold.at[:, UNITS[g][0] : UNITS[g][-1]], hold.at[:, UNITS[g][0] : UNITS[g][-1]],
+                    hold_send.at[g], hold_recv.at[g], device_id={"band": FROM, "col": c}, device_id_type=MESH,
+                ).wait_recv()
+                copy.start()
 
     def finish(pairs):
         for copy, way in pairs:
@@ -218,29 +283,8 @@
             pl.when(exists(*way))(copy.wait_send)
 
     waits = {}
-    arrive(0)
-    for g in range(len(UNITS)):
-        lo, hi = UNITS[g][0], UNITS[g][-1]
-        tile = DONE.get(g)
-        if g + 1 < len(UNITS):
-            arrive(g + 1)
-        down, upward = relays(g)
-        pl.when(b > 0)(down.wait_recv)
-        pl.when(b < NB - 1)(upward.wait_recv)
-
-        def rows_of(n, carry):
-            at_n = pl.ds(pl.multiple_of(lo + n * 256, 256), 256)
-            xh, xl = split(ext[:, at_n])
-            part = dot3(rh[...], rl[...], xh, xl)
-            high, low = split(part)
-            wh[:, at_n] = high
-            wl[:, at_n] = low
-            return carry
-
-        lax.fori_loop(0, (hi - lo) // 256, rows_of, 0)
-        if tile is None:
-            continue
-
+
+    def complete(tile):
         def cols_of(n, carry):
             at_n = pl.ds(pl.multiple_of(n * 256, 256), 256)
             part = dot3(wh[:, tile * TILE : tile * TILE + SPAN], wl[:, tile * TILE : tile * TILE + SPAN], ch[tile, :, at_n], cl[tile, :, at_n])
@@ -272,22 +316,46 @@
             pl.when(exists(*way))(copy.start)
         waits[tile] = pairs
 
-        if tile not in HORN:
-            continue
-        ready, spans = HORN[tile]
-        finish(waits.pop(ready))
-        if ready == 3:
-            z[8 : 8 + TILE, 0:MARGIN] = jnp.transpose(left[...])
-            z[8 : 8 + TILE, EXT - MARGIN : EXT] = jnp.transpose(right[...])
-
-        def strip(i, carry):
-            r = pl.multiple_of(i * 16, 16)
-            for first_col, last_col in spans:
-                o = (pl.ds(r, 16), slice(first_col, last_col))
-                vs[o], vh[o] = horn(z, inv, r, first_col, last_col - first_col)
-            return carry
-
-        lax.fori_loop(0, TILE // 16, strip, 0)
+    def main_rows(g):
+        lo, hi = UNITS[g][0], UNITS[g][-1]
+        xh, xl = split(ext[0:TILE, lo:hi])
+        acc[g % 2] = dot3(rh[:, 0:TILE], rl[:, 0:TILE], xh, xl)
+
+    arrive(0)
+    main_rows(0)
+    for g in range(len(UNITS)):
+        lo, hi = UNITS[g][0], UNITS[g][-1]
+        tile = DONE.get(g)
+        if g + 1 < len(UNITS):
+            forward(g)
+            arrive(g + 1)
+            main_rows(g + 1)
+        down, upward = relays(g)
+        pl.when(b > 0)(down.wait_recv)
+        pl.when(b < NB - 1)(upward.wait_recv)
+
+        xh, xl = split(ext[TILE:, lo:hi])
+        part = acc[g % 2] + dot3(rh[:, TILE:], rl[:, TILE:], xh, xl)
+        wh[:, lo:hi], wl[:, lo:hi] = split(part)
+        if g in MAKE:
+            make(MAKE[g])
+        if tile is not None:
+            complete(tile)
+        if g in HORN:
+            ready, spans = HORN[g]
+            finish(waits.pop(ready))
+            if ready == NT - 1:
+                z[8 : 8 + TILE, 0:MARGIN] = jnp.transpose(left[...])
+                z[8 : 8 + TILE, EXT - MARGIN : EXT] = jnp.transpose(right[...])
+
+            def strip(i, carry):
+                r = pl.multiple_of(i * 16, 16)
+                for first_col, last_col in spans:
+                    o = (pl.ds(r, 16), slice(first_col, last_col))
+                    vs[o], vh[o] = horn(z, inv, r, first_col, last_col - first_col)
+                return carry
+
+            lax.fori_loop(0, TILE // 16, strip, 0)
 
     for pairs in waits.values():
         finish(pairs)
@@ -300,6 +368,9 @@
         down, upward = relays(g)
         pl.when(b < NB - 1)(down.wait_send)
         pl.when(b > 0)(upward.wait_send)
+        if g + 1 < len(UNITS):
+            for chosen, copy in forwards(g):
+                pl.when(chosen)(copy.wait_send)
 
 
 def write_kernel(spacing, z, vs, vh, oz, osl, ohi, hs, hh, sem, late_sem):
@@ -347,11 +418,11 @@
             vmem((NT, SPAN, TILE), BF16), vmem((NT, SPAN, TILE), BF16),
             vmem((TILE, EXT), BF16), vmem((TILE, EXT), BF16),
             vmem((MARGIN, TILE), F32), vmem((MARGIN, TILE), F32),
-            vmem((8, TILE), F32), vmem((8, TILE), F32),
+            vmem((8, TILE), F32), vmem((8, TILE), F32), vmem((SLICE, EXT), F32), vmem((2, TILE, WIDE), F32),
             dma((nu,)), dma((nu, NC)), dma((nu,)), dma((2,)),
             dma((nu,)), dma((nu,)), dma((nu,)), dma((nu,)),
             dma((NT,)), dma((NT,)), dma((NT,)), dma((NT,)),
-            dma((2,)), dma((2,)), dma((4,)), dma((4,)),
+            dma((2,)), dma((2,)), dma((4,)), dma((4,)), dma((nu,)), dma((nu,)),
         ],
         compiler_params=pltpu.CompilerParams(
             collective_id=0, has_side_effects=True, vmem_limit_bytes=KERNEL_VMEM

time: 103 us -> 92.2 us (0.90)
  the two profiles are of different devices: /device:TPU:109 before, /device:TPU:71 now
where the time goes in v2:
time: 92.2 us; the launch traced here: 92 us
  Pallas kernels  90.1 us (98%)
  between operations  1.93 us (2%)
    pallas_call x1, Pallas kernels, on_device(): pl.pallas_call(gather_kernel, out_shape=(vmem((Z, EXT), F32), vmem((TILE,...  84.1 us
    pallas_call x1, Pallas kernels, on_device(): pl.pallas_call(write_kernel, out_shape=(out,) * 3, in_specs=[smem] + [in_...  6.02 us

profile of v2, /device:TPU:71, one launch (start us, length us, event | category | flops | bytes accessed | tf_op | source)
XLA Modules:
  0.0 92.0 jit_solution(3146621206736678639)
XLA Ops:
  1.9 84.1 %shard_map.85 = (f32[528,2304]{1,0:T(8,128)S(1)}, f32[512,2048]{1,0:T(8,128)S(1)}, f32[512,2048]{1,0:T(8,128)S(1)}) custom-call(s32[1]{0:T(128)S(6)} %copy.9.row_start, s32[4]{0:T(128)} %col_start.1, f32[1]{0:T(128)S(6)} %copy.10.spacing, f32[64,16384]{1,0:T(8,128)} %bands.1, f32[1,512,640]{2,1,0:T(8,128)} %row_interp.1, f32[4,640,512]{2,1,0:T(8,128)} %col_interp.1), custom_call_target="tpu_custom_call" | custom-call | tf_op jit(solution)/shard_map/pallas_call | solution.py:409
  86.0 6.0 %shard_map.86 = (f32[512,2048]{1,0:T(8,128)}, f32[512,2048]{1,0:T(8,128)}, f32[512,2048]{1,0:T(8,128)}) custom-call(f32[1]{0:T(128)S(6)} %copy.10.spacing, f32[528,2304]{1,0:T(8,128)S(1)} %get-tuple-element.6.z, f32[512,2048]{1,0:T(8,128)S(1)} %get-tuple-element.7.vs, f32[512,2048]{1,0:T(8,128)S(1)} %get-tuple-element.8.vh), custom_call_target="tpu_custom_call" | custom-call | tf_op jit(solution)/shard_map/pallas_call | solution.py:431

commit v3 on v2

--- a/solution.py
+++ b/solution.py
@@ -29,6 +29,7 @@
     (1280, 1536),
 )
 WIDE = 256
+STRIP = 32
 AHEAD = 2
 DONE = {2: 0, 5: 3, 7: 1, 8: 2}
 MAKE = {0: 0, 1: 3, 2: 1, 3: 2}
@@ -58,8 +59,8 @@
 
 def horn(z, inv, r, lo, width):
     span = width + 2 * MARGIN
-    blk = z[pl.ds(r, 32), lo : lo + span]
-    up, mid, dn = blk[7:23], blk[8:24], blk[9:25]
+    blk = z[pl.ds(r, STRIP + 16), lo : lo + span]
+    up, mid, dn = (blk[k : k + STRIP] for k in (7, 8, 9))
     s = up + dn + 2.0 * mid
     d = dn - up
     sc = jnp.tile(inv, (1, width // 128))
@@ -73,7 +74,7 @@
 
 
 def inverse(spacing):
-    return 1.0 / jnp.full((16, 128), 8.0 * spacing[0], F32)
+    return 1.0 / jnp.full((STRIP, 128), 8.0 * spacing[0], F32)
 
 
 def gather_kernel(
@@ -349,13 +350,13 @@
                 z[8 : 8 + TILE, EXT - MARGIN : EXT] = jnp.transpose(right[...])
 
             def strip(i, carry):
-                r = pl.multiple_of(i * 16, 16)
+                r = pl.multiple_of(i * STRIP, STRIP)
                 for first_col, last_col in spans:
-                    o = (pl.ds(r, 16), slice(first_col, last_col))
+                    o = (pl.ds(r, STRIP), slice(first_col, last_col))
                     vs[o], vh[o] = horn(z, inv, r, first_col, last_col - first_col)
                 return carry
 
-            lax.fori_loop(0, TILE // 16, strip, 0)
+            lax.fori_loop(0, TILE // STRIP, strip, 0)
 
     for pairs in waits.values():
         finish(pairs)
@@ -384,14 +385,14 @@
     parts = 4
     for part in range(parts):
         def strip(i, carry):
-            r = pl.multiple_of(i * 16, 16)
+            r = pl.multiple_of(i * STRIP, STRIP)
             for lo in range(LATE[0], LATE[1], 384):
-                o = (pl.ds(r, 16), slice(lo - LATE[0], lo - LATE[0] + 384))
+                o = (pl.ds(r, STRIP), slice(lo - LATE[0], lo - LATE[0] + 384))
                 hs[o], hh[o] = horn(z, inv, r, lo, 384)
             return carry
 
         first, last = part * TILE // parts, (part + 1) * TILE // parts
-        lax.fori_loop(first // 16, last // 16, strip, 0)
+        lax.fori_loop(first // STRIP, last // STRIP, strip, 0)
         for k, (v, o) in enumerate(((hs, osl), (hh, ohi))):
             copy = pltpu.make_async_copy(v.at[first:last], o.at[first:last, LATE[0] : LATE[1]], late_sem.at[k, part])
             copy.start()

time: 92.2 us -> 88.8 us (0.963)
  Pallas kernels: 90.1 us -> 86.6 us
    pallas_call x1, Pallas kernels: 84.1 us -> 81.8 us  [on_device(): pl.pallas_call(gather_kernel, out_shape=(vmem((Z, EXT), F32), vmem((TILE,...]
    pallas_call x1, Pallas kernels: 6.02 us -> 4.73 us  [on_device(): pl.pallas_call(write_kernel, out_shape=(out,) * 3, in_specs=[smem] + [in_...]
where the time goes in v3:
time: 88.8 us; the launch traced here: 88.7 us
  Pallas kernels  86.6 us (98%)
  between operations  2.09 us (2%)
    pallas_call x1, Pallas kernels, on_device(): pl.pallas_call(gather_kernel, out_shape=(vmem((Z, EXT), F32), vmem((TILE,...  81.8 us
    pallas_call x1, Pallas kernels, on_device(): pl.pallas_call(write_kernel, out_shape=(out,) * 3, in_specs=[smem] + [in_...  4.73 us

profile of v3, /device:TPU:71, one launch (start us, length us, event | category | flops | bytes accessed | tf_op | source)
XLA Modules:
  0.0 88.7 jit_solution(6668856100495565830)
XLA Ops:
  1.9 81.8 %shard_map.85 = (f32[528,2304]{1,0:T(8,128)S(1)}, f32[512,2048]{1,0:T(8,128)S(1)}, f32[512,2048]{1,0:T(8,128)S(1)}) custom-call(s32[1]{0:T(128)S(6)} %copy.9.row_start, s32[4]{0:T(128)} %col_start.1, f32[1]{0:T(128)S(6)} %copy.10.spacing, f32[64,16384]{1,0:T(8,128)} %bands.1, f32[1,512,640]{2,1,0:T(8,128)} %row_interp.1, f32[4,640,512]{2,1,0:T(8,128)} %col_interp.1), custom_call_target="tpu_custom_call" | custom-call | tf_op jit(solution)/shard_map/pallas_call | solution.py:410
  83.8 4.7 %shard_map.86 = (f32[512,2048]{1,0:T(8,128)}, f32[512,2048]{1,0:T(8,128)}, f32[512,2048]{1,0:T(8,128)}) custom-call(f32[1]{0:T(128)S(6)} %copy.10.spacing, f32[528,2304]{1,0:T(8,128)S(1)} %get-tuple-element.6.z, f32[512,2048]{1,0:T(8,128)S(1)} %get-tuple-element.7.vs, f32[512,2048]{1,0:T(8,128)S(1)} %get-tuple-element.8.vh), custom_call_target="tpu_custom_call" | custom-call | tf_op jit(solution)/shard_map/pallas_call | solution.py:432
